TPU v7x, 32 devices: a whole 2x2x4 slice. The times are simulated.
32 devices in a mesh: dp: 4 (over y, core), fsdp: 8 (over z, x).
Axes of the slice: x: 2, y: 2, z: 4, core: 2. Of those that a mesh axis runs over, the one named last changes fastest.
Arguments:
- hidden_in: bfloat16 [20480, 768], P(('dp', 'fsdp')), may hold values from -7 to 7
- prev_logits: bfloat16 [32, 12, 640, 640], P(('dp', 'fsdp')), may hold values from -6 to 6
- segment_ids: int32 [32, 640], P(('dp', 'fsdp')), may hold values from 0 to 3, never falling along the last dimension, each value on 1 to 320 neighbouring positions
- d_hidden: bfloat16 [20480, 768], P(('dp', 'fsdp')), may hold values from -6 to 6
- d_logits: bfloat16 [32, 12, 640, 640], P(('dp', 'fsdp')), may hold values from -3 to 3
- weight_in: float32 [768, 5376], P(('dp', 'fsdp')), may hold values from -2.5 to 2.5
- weight_out: float32 [3840, 768], P(('dp', 'fsdp')), may hold values from -2 to 2
- vectors: float32 [12, 768], P(None, ('dp', 'fsdp')), may hold values from -0.6 to 1.45
- moment_in: float32 [768, 5376], P(('dp', 'fsdp')), may hold values from -0.55 to 0.55
- moment_out: float32 [3840, 768], P(('dp', 'fsdp')), may hold values from -0.55 to 0.55
- moment_vectors: float32 [12, 768], P(None, ('dp', 'fsdp')), may hold values from -1.5 to 1.5
- square_in: float32 [768, 5376], P(('dp', 'fsdp')), may hold values from 0.001 to 0.004
- square_out: float32 [3840, 768], P(('dp', 'fsdp')), may hold values from 0.001 to 0.004
- square_vectors: float32 [12, 768], P(None, ('dp', 'fsdp')), may hold values from 0.008 to 0.032
- step_count: int32 [1], replicated, may hold values from 1 to 20
Outputs:
- hidden_out: bfloat16 [20480, 768], P(('dp', 'fsdp'))
- logits: bfloat16 [32, 12, 640, 640], P(('dp', 'fsdp'))
- d_input: bfloat16 [20480, 768], P(('dp', 'fsdp'))
- d_prev: bfloat16 [32, 12, 640, 640], P(('dp', 'fsdp'))
- grad_weight_in: float32 [768, 5376], P(('dp', 'fsdp'))
- grad_weight_out: float32 [3840, 768], P(('dp', 'fsdp'))
- grad_vectors: float32 [12, 768], P(None, ('dp', 'fsdp'))
- new_moment_in: float32 [768, 5376], P(('dp', 'fsdp'))
- new_moment_out: float32 [3840, 768], P(('dp', 'fsdp'))
- new_moment_vectors: float32 [12, 768], P(None, ('dp', 'fsdp'))
- new_square_in: float32 [768, 5376], P(('dp', 'fsdp'))
- new_square_out: float32 [3840, 768], P(('dp', 'fsdp'))
- new_square_vectors: float32 [12, 768], P(None, ('dp', 'fsdp'))
- new_weight_in: float32 [768, 5376], P(('dp', 'fsdp'))
- new_weight_out: float32 [3840, 768], P(('dp', 'fsdp'))
- new_vectors: float32 [12, 768], P(None, ('dp', 'fsdp'))
- copy_weight_in: bfloat16 [768, 5376], P(('dp', 'fsdp'))
- copy_weight_out: bfloat16 [3840, 768], P(('dp', 'fsdp'))
- copy_vectors: bfloat16 [12, 768], P(None, ('dp', 'fsdp'))
- grad_norm: float32 [], replicated
Inputs may be any that keep to these rules, and one draw needn't show every extreme that they name: `segment_ids`: along each row the segment numbers never fall; no segment holds more than 320 slots.
All inputs are finite; a program needn't handle non-finite values.
Results may differ from a plain program's by a relative error of at most 0.012.
Values may be sent and summed in bfloat16 or wider, within the bound.
A program may use at most 192 MiB of HBM per device.

v0:
```python
import functools
import math

import jax
import jax.numpy as jnp
from jax import lax
from jax.experimental import pallas as pl
from jax.experimental.pallas import tpu as pltpu
from jax.sharding import PartitionSpec as P

PARAMS = 7087104


norm_eps = 1e-12
clip_scale = 1.0
beta_one = 0.9
beta_two = 0.999
adam_eps = 1e-08
rate_matrix = 0.06
rate_vector = 0.25
decay_matrix = 0.01
NEG = -1e30
NT = (((1,), (1,)), ((), ()))
NN = (((1,), (0,)), ((), ()))
TN = (((0,), (0,)), ((), ()))
AXES = ("dp", "fsdp")


def gelu_exact(upward):
    return jax.nn.gelu(upward, approximate=False)


def norm_rows(residual, gain_row, shift_row):
    centered = residual - jnp.mean(residual, axis=1, keepdims=True)
    scaling = lax.rsqrt(jnp.mean(centered * centered, axis=1, keepdims=True) + norm_eps)
    normed = centered * scaling
    return (normed * gain_row + shift_row, normed, scaling)


def norm_back(grad_after, normed, scaling, gain_row):
    scaled_grad = grad_after * gain_row
    return scaling * (
        scaled_grad
        - jnp.mean(scaled_grad, axis=1, keepdims=True)
        - normed * jnp.mean(scaled_grad * normed, axis=1, keepdims=True)
    )


def dotf(a, b, dims):
    return lax.dot_general(a, b, dims, preferred_element_type=jnp.float32)

def half_masks(rows):
    lane = lax.broadcasted_iota(jnp.int32, (rows, 128), 1)
    return lane < 64

def attn_fwd_kernel(BR, q_ref, k_ref, v_ref, prev_ref, srow_ref, scol_ref, logits_ref, mixed_ref, lse_ref, mask_ref):
    g = pl.program_id(0)
    rows = q_ref.shape[0]
    @pl.when(g == 0)
    def _():
        mask_ref[...] = jnp.where(scol_ref[...] == srow_ref[...], 0.0, NEG)
        lse_ref[...] = jnp.zeros_like(lse_ref)
    k2 = k_ref[...]
    v2 = v_ref[...]
    left = half_masks(rows)
    zero = jnp.zeros_like(v2)
    va = jnp.where(left, v2, zero)
    vb = jnp.where(left, zero, v2)
    for rb in range(rows // BR):
        sl = pl.ds(rb * BR, BR)
        q2 = q_ref[sl, :] * jnp.bfloat16(0.125)
        lb = half_masks(BR)
        outs = []
        lses = []
        for h in range(2):
            qh = jnp.where(lb if h == 0 else ~lb, q2, jnp.zeros_like(q2))
            raw = dotf(qh, k2, NT) + prev_ref[h, sl, :].astype(jnp.float32)
            logits_ref[h, sl, :] = raw.astype(jnp.bfloat16)
            s = raw + mask_ref[sl, :]
            m = jnp.max(s, axis=1, keepdims=True)
            e = jnp.exp(s - m)
            tot = jnp.sum(e, axis=1, keepdims=True)
            o = dotf(e.astype(jnp.bfloat16), va if h == 0 else vb, NN)
            outs.append(o / tot)
            lses.append(m + jnp.log(tot))
        mixed_ref[sl, :] = (outs[0] + outs[1]).astype(jnp.bfloat16)
        lane = lax.broadcasted_iota(jnp.int32, (BR, 128), 1)
        cur = lse_ref[sl, :]
        cur = jnp.where(lane == 2 * g, lses[0], cur)
        cur = jnp.where(lane == 2 * g + 1, lses[1], cur)
        lse_ref[sl, :] = cur

def attn_fwd(qkv, prev, seg, BR=128):
    rows = qkv.shape[0]
    heads = prev.shape[0]
    G = heads // 2
    srow = seg.reshape(1, rows); scol = seg.reshape(rows, 1)
    return pl.pallas_call(
        functools.partial(attn_fwd_kernel, BR),
        grid=(G,),
        in_specs=[
            pl.BlockSpec((rows, 128), lambda g: (0, g)),
            pl.BlockSpec((rows, 128), lambda g: (0, G + g)),
            pl.BlockSpec((rows, 128), lambda g: (0, 2 * G + g)),
            pl.BlockSpec((2, rows, rows), lambda g: (g, 0, 0)),
            pl.BlockSpec((1, rows), lambda g: (0, 0)),
            pl.BlockSpec((rows, 1), lambda g: (0, 0)),
        ],
        out_specs=[
            pl.BlockSpec((2, rows, rows), lambda g: (g, 0, 0)),
            pl.BlockSpec((rows, 128), lambda g: (0, g)),
            pl.BlockSpec((rows, 128), lambda g: (0, 0)),
        ],
        out_shape=[
            jax.ShapeDtypeStruct((heads, rows, rows), jnp.bfloat16),
            jax.ShapeDtypeStruct((rows, heads * 64), jnp.bfloat16),
            jax.ShapeDtypeStruct((rows, 128), jnp.float32),
        ],
        scratch_shapes=[pltpu.VMEM((rows, rows), jnp.float32)],
        compiler_params=pltpu.CompilerParams(vmem_limit_bytes=60 * 2**20),
        name="attn_fwd",
    )(qkv, qkv, qkv, prev, srow, scol)

def attn_bwd_kernel(BR, q_ref, k_ref, v_ref, do_ref, prev_ref, dl_ref, lse_ref, srow_ref, scol_ref,
                    dprev_ref, dq_ref, dk_ref, dv_ref, mask_ref, p_ref, g_ref):
    g = pl.program_id(0)
    rows = q_ref.shape[0]
    @pl.when(g == 0)
    def _():
        mask_ref[...] = jnp.where(scol_ref[...] == srow_ref[...], 0.0, NEG)
    k2 = k_ref[...]
    v2 = v_ref[...]
    left = half_masks(rows)
    zero = jnp.zeros_like(v2)
    for h in range(2):
        lm = left if h == 0 else ~left
        kh = jnp.where(lm, k2, zero)
        for rb in range(rows // BR):
            sl = pl.ds(rb * BR, BR)
            lb = half_masks(BR)
            lb = lb if h == 0 else ~lb
            q2 = q_ref[sl, :] * jnp.bfloat16(0.125)
            qh = jnp.where(lb, q2, jnp.zeros_like(q2))
            doh = jnp.where(lb, do_ref[sl, :], jnp.zeros_like(q2))
            lane = lax.broadcasted_iota(jnp.int32, (BR, 128), 1)
            lse = jnp.sum(jnp.where(lane == 2 * g + h, lse_ref[sl, :], 0.0), axis=1, keepdims=True)
            s = dotf(qh, k2, NT) + prev_ref[h, sl, :].astype(jnp.float32) + mask_ref[sl, :]
            p = jnp.exp(s - lse)
            dp = dotf(doh, v2, NT)
            delta = jnp.sum(p * dp, axis=1, keepdims=True)
            ds = p * (dp - delta)
            gt = (ds + dl_ref[h, sl, :].astype(jnp.float32)).astype(jnp.bfloat16)
            dprev_ref[h, sl, :] = gt
            p_ref[sl, :] = p.astype(jnp.bfloat16)
            dq = dotf(gt, kh, NN) * 0.125
            if h == 0:
                dq_ref[sl, :] = dq.astype(jnp.bfloat16)
            else:
                dq_ref[sl, :] = dq_ref[sl, :] + dq.astype(jnp.bfloat16)
        qh = jnp.where(lm, q_ref[...], zero)
        doh = jnp.where(lm, do_ref[...], zero)
        dk = (dotf(dprev_ref[h], qh, TN) * 0.125).astype(jnp.bfloat16)
        dv = dotf(p_ref[...], doh, TN).astype(jnp.bfloat16)
        if h == 0:
            dk_ref[...] = dk
            dv_ref[...] = dv
        else:
            dk_ref[...] = dk_ref[...] + dk
            dv_ref[...] = dv_ref[...] + dv

def attn_bwd(qkv, do, prev, dl, lse, seg, BR=128):
    rows = qkv.shape[0]
    heads = prev.shape[0]
    G = heads // 2
    srow = seg.reshape(1, rows); scol = seg.reshape(rows, 1)
    col = lambda off: pl.BlockSpec((rows, 128), lambda g: (0, off + g))
    return pl.pallas_call(
        functools.partial(attn_bwd_kernel, BR),
        grid=(G,),
        in_specs=[
            col(0), col(G), col(2 * G), col(0),
            pl.BlockSpec((2, rows, rows), lambda g: (g, 0, 0)),
            pl.BlockSpec((2, rows, rows), lambda g: (g, 0, 0)),
            pl.BlockSpec((rows, 128), lambda g: (0, 0)),
            pl.BlockSpec((1, rows), lambda g: (0, 0)),
            pl.BlockSpec((rows, 1), lambda g: (0, 0)),
        ],
        out_specs=[
            pl.BlockSpec((2, rows, rows), lambda g: (g, 0, 0)),
            col(0), col(0), col(0),
        ],
        out_shape=[
            jax.ShapeDtypeStruct((heads, rows, rows), jnp.bfloat16),
        ] + [jax.ShapeDtypeStruct((rows, heads * 64), jnp.bfloat16)] * 3,
        scratch_shapes=[pltpu.VMEM((rows, rows), jnp.float32), pltpu.VMEM((rows, rows), jnp.bfloat16), pltpu.VMEM((8, 128), jnp.float32)],
        compiler_params=pltpu.CompilerParams(vmem_limit_bytes=60 * 2**20),
        name="attn_bwd",
    )(qkv, qkv, qkv, do, prev, dl, lse, srow, scol)


MESH = pl.DeviceIdType.MESH


def coords():
    dp = lax.axis_index("dp"); fs = lax.axis_index("fsdp")
    y = dp // 2; c = lax.rem(dp, 2)
    z = fs // 2; x = lax.rem(fs, 2)
    return y, c, z, x

def dev(y, c, z, x):
    return (y * 2 + c, z * 2 + x)


ROUTES = "zzzzzzznnnn"
FORWARD_PLAN = {
    "start": [(1, 7), (1, 8), (1, 9), (1, 10), (1, 0), (2, 0), (1, 1), (3, 0)],
    ("q", 0): [(1, 2), (2, 1), (1, 3), (2, 2), (3, 1)],
    ("q", 1): [(2, 3), (1, 4), (3, 2)],
    ("q", 2): [(3, 3), (1, 5)],
    ("pair", 0): [(2, 4), (1, 6)],
    ("pair", 2): [(2, 5)],
    ("pair", 3): [(3, 4)],
    ("pair", 5): [(2, 6)],
    "out": [(3, 5), (2, 7), (3, 6), (2, 8)],
    "norm": [(3, 7), (2, 9)],
    ("up", 0): [(3, 8), (2, 10)],
    ("up", 1): [(3, 9)],
    ("up", 2): [(3, 10)],
}
BACKWARD_PLAN = {
    ("up", 1): [(2, 0)],
    ("down", 2): [(2, 1)],
    ("down", 3): [(3, 0), (2, 2)],
    "norm": [(3, 1), (4, 0), (2, 3)],
    "out": [(4, 1), (3, 2)],
    ("head", 0): [(3, 3), (5, 0)],
    ("head", 2): [(4, 2), (4, 3), (2, 4), (2, 5), (5, 1)],
    ("head", 3): [(2, 6), (2, 7)],
    ("head", 4): [(5, 2)],
    ("head", 5): [(3, 4)],
    ("head", 6): [(2, 8), (5, 3)],
    ("head", 7): [(3, 5)],
    ("head", 8): [(2, 9)],
    ("head", 9): [(3, 6)],
    ("head", 10): [(3, 7), (2, 10), (4, 4)],
    ("head", 11): [(3, 8), (2, 11)],
    "end": [(4, 5), (3, 9)],
    ("dx", 1): [(4, 6), (4, 7), (2, 12), (2, 13), (3, 10), (5, 4)],
    "last": [(4, 8), (4, 9), (3, 11), (3, 12), (5, 5), (3, 13), (4, 10), (4, 11), (4, 12), (4, 13), (5, 6), (5, 7), (5, 8), (5, 9), (5, 10), (5, 11), (5, 12), (5, 13)],
}


class Gather:
    def __init__(self, chunks, routes, sources, wholes, send_sem, recv_sem):
        self.chunks, self.routes, self.sources, self.wholes = chunks, routes, sources, wholes
        self.send_sem, self.recv_sem = send_sem, recv_sem
        self.y, self.c, self.z, self.x = coords()

    def part(self, k):
        array, start, size, origin = self.chunks[k]
        return self.wholes[array], pl.ds(start, size), self.sources[array].at[:, pl.ds(origin, size)]

    def rows_of(self, k, x):
        size = self.sources[self.chunks[k][0]].shape[0]
        return pl.ds(pl.multiple_of(size * x, 8), size)

    def copy(self, src, dst, k, slot, who):
        return pltpu.make_async_remote_copy(
            src_ref=src, dst_ref=dst, send_sem=self.send_sem.at[k, slot], recv_sem=self.recv_sem.at[k, slot],
            device_id=who, device_id_type=MESH)

    def along_z(self, k):
        whole, cols, mine = self.part(k)
        spot = whole.at[self.y, self.c, self.z, self.rows_of(k, self.x), cols]
        return [self.copy(mine, spot, k, d, dev(self.y, self.c, lax.rem(self.z + d + 1, 4), self.x)) for d in range(3)]

    def across(self):
        return jnp.where(self.c == 0, self.y, 1 - self.y), jnp.where(self.c == 0, 1 - self.x, self.x)

    def other(self):
        return (jnp.where(self.c == 0, 1 - self.y, self.y) * 2 + self.c, self.z * 2 + jnp.where(self.c == 0, self.x, 1 - self.x))

    def block(self, k, y, x):
        whole, cols, _ = self.part(k)
        return whole.at[y, self.c, :, self.rows_of(k, x), cols]

    def to_neighbours(self, k):
        block = self.block(k, self.y, self.x)
        return [self.copy(block, block, k, 3, dev(self.y, self.c, self.z, 1 - self.x)),
                self.copy(block, block, k, 4, dev(1 - self.y, self.c, self.z, self.x))]

    def handed_on(self, k):
        block = self.block(k, *self.across())
        return self.copy(block, block, k, 3 + self.c, self.other()), self.copy(block, block, k, 5, self.other()), self.copy(block, block, k, 4 - self.c, self.other())

    def early(self, k):
        whole, cols, mine = self.part(k)
        y, x = self.across()
        return self.copy(mine, whole.at[self.y, self.c, self.z, self.rows_of(k, self.x), cols], k, 3, dev(y, self.c, self.z, x))

    def relayed(self, k):
        whole, cols, _ = self.part(k)
        y, x = self.across()
        spot = whole.at[y, self.c, self.z, self.rows_of(k, x), cols]
        return [self.copy(spot, spot, k, 4 + d, dev(self.y, self.c, lax.rem(self.z + d + 1, 4), self.x)) for d in range(3)]

    def halves(self, k):
        own, far = self.block(k, self.y, self.x), self.block(k, *self.across())
        return [self.copy(own, own, k, 7, self.other()), self.copy(far, far, k, 8, self.other())]

    def to_core(self, k):
        whole, cols, _ = self.part(k)
        plane = whole.at[:, self.c, :, :, cols]
        return self.copy(plane, plane, k, 9, dev(self.y, 1 - self.c, self.z, self.x))

    def start(self, k):
        if self.routes[k] == "n":
            self.early(k).start()
        for d in self.along_z(k):
            d.start()

    def s1(self, k):
        if self.routes[k] == "n":
            self.early(k).wait_recv()
            for d in self.relayed(k):
                d.start()
            return
        for d in self.along_z(k):
            d.wait_recv()
        for d in self.to_neighbours(k):
            d.start()

    def s2(self, k):
        if self.routes[k] == "n":
            for d in self.along_z(k) + self.relayed(k):
                d.wait_recv()
            for d in self.halves(k):
                d.start()
            return
        got, on, _ = self.handed_on(k)
        got.wait_recv()
        on.start()

    def s3(self, k):
        if self.routes[k] == "n":
            for d in self.halves(k):
                d.wait_recv()
        else:
            _, on, other = self.handed_on(k)
            other.wait_recv()
            on.wait_recv()
        self.to_core(k).start()

    def s4(self, k):
        self.to_core(k).wait_recv()

    def finish(self, k):
        if self.routes[k] == "n":
            sent = [self.early(k), *self.relayed(k), *self.halves(k)]
        else:
            sent = self.to_neighbours(k) + [self.handed_on(k)[1]]
        for d in self.along_z(k) + sent + [self.to_core(k)]:
            d.wait_send()


def peers_of(y, c, z, x):
    return [dev(y, c, lax.rem(z + d, 4), x) for d in (1, 2, 3)] + [dev(y, c, z, 1 - x), dev(1 - y, c, z, x), dev(y, 1 - c, z, x)]


def normalise(v):
    centered = v - jnp.mean(v, axis=1, keepdims=True)
    scaling = lax.rsqrt(jnp.mean(centered * centered, axis=1, keepdims=True) + norm_eps)
    return centered * scaling, scaling


def spread_columns(ref, shards, columns, rows, width):
    lane = lax.broadcasted_iota(jnp.int32, (rows, 128), 1)
    blocks = [jnp.zeros((rows, 128), jnp.float32) for _ in range(width // 128)]
    for d in range(shards):
        at, off = columns * d // 128, columns * d % 128
        tile = ref[d // 16, d // 8 % 2, d // 2 % 4, 16 * (d % 2):16 * (d % 2) + 16, :][:rows]
        tile = pltpu.roll(tile, off, 1) if off else tile
        if off + columns > 128:
            blocks[at + 1] = blocks[at + 1] + jnp.where(lane < off, tile, 0.0)
            tile = jnp.where(lane < off, 0.0, tile)
        blocks[at] = blocks[at] + tile
    return blocks


def forward_kernel(plan, routes, win_ref, wout_ref, vec_ref, srow_ref, prev_ref, x_hbm, dout_hbm,
                   logits_ref, probs_ref, gq_ref, gu_ref, go_ref, qkv_hbm, mixed_hbm, hlow_hbm, none_hbm, act_hbm, gp_hbm,
                   small_ref, sone_ref, out_ref, dsec_ref, ddown_ref, sums_ref,
                   gv_ref, mask_ref, cin_ref, cout_ref, cvec_ref, w_ref, wo_ref, x_ref, dout_ref, qkv_ref, mixed_ref, hlow_ref, none_ref,
                   act_ref, gp_ref, hid_ref, sec_ref, send_sem, recv_sem, loc_sem, out_sem):
    g = pl.program_id(0)
    rows, width = x_hbm.shape
    hidden = act_hbm.shape[1]
    last = pl.num_programs(0) - 1
    tile = 256
    y, c, z, x = coords()
    V, Q, O, U = 0, 1, 4, 7
    chunks = [(3, 0, 128, 0)] + [(0, 768 * i, 768, 768 * i) for i in range(3)] + [(2, 256 * i, 256, 256 * i) for i in range(3)]
    chunks += [(1, 768 * i, 768, 3 * width + 768 * i) for i in range(4)]
    ga = Gather(chunks, routes, [cin_ref, cin_ref, cout_ref, cvec_ref], [gq_ref, gu_ref, go_ref, gv_ref], send_sem, recv_sem)

    def run(place):
        for stage, k in plan.get(place, ()):
            (ga.s1, ga.s2, ga.s3)[stage - 1](k)

    def load(src, dst, i):
        return pltpu.make_async_copy(src, dst, loc_sem.at[i])

    def save(src, dst, i):
        return pltpu.make_async_copy(src, dst, out_sem.at[i])

    stores = lambda: [load(cin_ref.at[:, pl.ds(0, 3 * width)], gq_ref.at[y, c, z, ga.rows_of(Q, x)], 0),
                      load(cin_ref.at[:, pl.ds(3 * width, hidden)], gu_ref.at[y, c, z, ga.rows_of(U, x)], 1),
                      load(cout_ref, go_ref.at[y, c, z, ga.rows_of(O, x)], 2)]
    x_in, dout_in = lambda: load(x_hbm, x_ref, 3), lambda: load(dout_hbm, dout_ref, 4)
    w_out, w_up, w_qkv = go_ref.reshape(width + hidden, width), gu_ref.reshape(width, hidden), gq_ref.reshape(width, 3 * width)
    w_q = lambda k: load(w_qkv.at[:, pl.ds(768 * k, 768)], w_ref.at[k % 2], 5 + k % 2)
    w_u = lambda k: load(w_up.at[:, pl.ds(768 * k, 768)], w_ref.at[(k + 1) % 2], 5 + (k + 1) % 2)
    w_o = lambda: load(w_out.at[pl.ds(0, width), :], w_ref.at[0], 5)
    w_down = lambda: load(w_out.at[pl.ds(width, hidden), :], wo_ref, 7)
    saves = {"mixed": lambda: save(mixed_ref, mixed_hbm, 1), "hlow": lambda: save(hlow_ref, hlow_hbm, 2),
             "none": lambda: save(none_ref, none_hbm, 3), "qkv": lambda: save(qkv_ref, qkv_hbm, 4)}
    save_act = lambda k: save(act_ref.at[:, pl.ds(768 * k, 768)], act_hbm.at[:, pl.ds(768 * k, 768)], 5 + k)
    save_gp = lambda k: save(gp_ref.at[k % 2], gp_hbm.at[:, pl.ds(768 * k, 768)], 9 + k)

    @pl.when(g == 0)
    def _():
        barrier = pltpu.get_barrier_semaphore()
        peers = peers_of(y, c, z, x)
        for p in peers:
            pl.semaphore_signal(barrier, inc=1, device_id=p, device_id_type=MESH)
        cvec_ref[...] = jnp.zeros_like(cvec_ref)
        vec = vec_ref[...].astype(jnp.bfloat16).astype(jnp.float32)
        cvec_ref[0:vec.shape[0], 0:vec.shape[1]] = vec
        gv_ref[y, c, z, ga.rows_of(V, x), :] = cvec_ref[...]
        cin_ref[...] = win_ref[...].astype(jnp.bfloat16)
        cout_ref[...] = wout_ref[...].astype(jnp.bfloat16)
        pl.semaphore_wait(barrier, len(peers))
        for k in range(len(chunks)):
            ga.start(k)
        for s in stores():
            s.start()
        x_in().start()
        seg = jnp.broadcast_to(srow_ref[...].astype(jnp.float32), (rows, rows))
        mask_ref[...] = jnp.where(seg == seg.T, 0.0, NEG)
        for s in stores():
            s.wait()
        dout_in().start()
        run("start")
        ga.s4(V)
        run("small")
        spread = spread_columns(gv_ref, 32, vec_ref.shape[1], vec_ref.shape[0], width)
        for i, v in enumerate(spread):
            small_ref[:, 128 * i:128 * (i + 1)] = v
        x_in().wait()

        @pl.loop(0, 3)
        def _(k):
            for i in range(3):
                @pl.when(k == i)
                def _():
                    run(("q", i))
                    ga.s4(Q + i)
                    w_q(i).start()
                    run(("qw", i))
                    w_q(i).wait()
            bias = jnp.where(k == 1, 0.0, small_ref[pl.ds(4 + k // 2, 1), :])
            v = dotf(x_ref[...], w_ref[lax.rem(k, 2)], NN) + bias
            qkv_ref[:, pl.ds(pl.multiple_of(768 * k, 768), 768)] = v.astype(jnp.bfloat16)
        saves["qkv"]().start()

    for i in range(6):
        if plan.get(("pair", i)):
            @pl.when(g == i)
            def _():
                run(("pair", i))

    at = lambda off: pl.ds(pl.multiple_of(off * width + g * 128, 128), 128)
    left = half_masks(rows)
    q2 = qkv_ref[:, at(0)] * jnp.bfloat16(0.125)
    k2 = qkv_ref[:, at(1)]
    v2 = qkv_ref[:, at(2)]
    zero = jnp.zeros_like(v2)
    outs = []
    for h in range(2):
        pick = (lambda v: jnp.where(left, v, zero)) if h == 0 else (lambda v: jnp.where(left, zero, v))
        raw = dotf(pick(q2), k2, NT) + prev_ref[h].astype(jnp.float32)
        logits_ref[h] = raw.astype(jnp.bfloat16)
        s = raw + mask_ref[...]
        e = jnp.exp(s - jnp.max(s, axis=1, keepdims=True))
        probs = (e * (1.0 / jnp.sum(e, axis=1, keepdims=True))).astype(jnp.bfloat16)
        probs_ref[h] = probs
        outs.append(dotf(probs, pick(v2), NN))
    mixed_ref[:, pl.ds(pl.multiple_of(g * 128, 128), 128)] = (outs[0] + outs[1]).astype(jnp.bfloat16)

    @pl.when(g == last)
    def _():
        saves["mixed"]().start()
        run("out")
        for k in range(3):
            ga.s4(O + k)
        w_o().start()
        w_down().start()
        run("outw")
        w_o().wait()
        hid_ref[...] = x_ref[...].astype(jnp.float32) + (dotf(mixed_ref[...], w_ref[0], NN) + small_ref[6:7, :])
        run("norm")

        @pl.loop(0, rows // 128)
        def _(i):
            sl = pl.ds(pl.multiple_of(i * 128, 128), 128)
            normed, scaling = normalise(hid_ref[sl, :])
            none_ref[sl, :] = normed
            sone_ref[sl, :] = jnp.broadcast_to(scaling, (128, 128))
            hid = normed * small_ref[0:1, :] + small_ref[2:3, :]
            hid_ref[sl, :] = hid
            hlow_ref[sl, :] = hid.astype(jnp.bfloat16)

        saves["none"]().start()
        saves["hlow"]().start()

        @pl.loop(0, 4)
        def _(k):
            for i in range(4):
                @pl.when(k == i)
                def _():
                    run(("up", i))
                    ga.s4(U + i)
                    w_u(i).start()
                    run(("upw", i))
                    w_u(i).wait()
                    if i >= 2:
                        save_gp(i - 2).wait()

            @pl.loop(0, 768 // tile)
            def _(j):
                sl = pl.ds(pl.multiple_of(j * tile, tile), tile)
                to = pl.ds(pl.multiple_of(768 * k + j * tile, tile), tile)
                u = dotf(hlow_ref[...], w_ref[lax.rem(k + 1, 2), :, sl], NN) + small_ref[pl.ds(8 + k, 1), sl]
                cdf = 0.5 * (1.0 + lax.erf(u * math.sqrt(0.5)))
                act_ref[:, to] = (u * cdf).astype(jnp.bfloat16)
                gp_ref[lax.rem(k, 2), :, sl] = (cdf + u * (jnp.exp(-0.5 * (u * u)) * (1.0 / math.sqrt(2.0 * math.pi)))).astype(jnp.bfloat16)
            for i in range(4):
                @pl.when(k == i)
                def _():
                    save_act(i).start()
                    save_gp(i).start()
        w_down().wait()
        sec_ref[...] = hid_ref[...] + (dotf(act_ref[...], wo_ref[...], NN) + small_ref[7:8, :])
        sums_ref[...] = jnp.zeros_like(sums_ref)
        dout_in().wait()

        @pl.loop(0, rows // 128)
        def _(i):
            sl = pl.ds(pl.multiple_of(i * 128, 128), 128)
            normed, scaling = normalise(sec_ref[sl, :])
            out_ref[sl, :] = (normed * small_ref[1:2, :] + small_ref[3:4, :]).astype(jnp.bfloat16)
            dy = dout_ref[sl, :].astype(jnp.float32)
            back = norm_back(dy, normed, scaling, small_ref[1:2, :])
            low = back.astype(jnp.bfloat16)
            dsec_ref[sl, :] = back
            ddown_ref[sl, :] = low
            sums_ref[0:1, :] += jnp.sum(dy * normed, axis=0, keepdims=True)
            sums_ref[1:2, :] += jnp.sum(dy, axis=0, keepdims=True)
            sums_ref[2:3, :] += jnp.sum(low.astype(jnp.float32), axis=0, keepdims=True)
        for k in range(len(chunks)):
            ga.finish(k)
        for s in saves.values():
            s().wait()
        for k in range(4):
            save_act(k).wait()
        for k in (2, 3):
            save_gp(k).wait()


def forward_all(plan, routes, tokens, grad_out, weight_in, weight_out, vectors, prev, seg):
    rows, width = tokens.shape
    heads = prev.shape[0]
    hidden = weight_in.shape[1] - 3 * width
    f32, bf16 = jnp.float32, jnp.bfloat16
    fixed = lambda shape: pl.BlockSpec(shape, lambda g: (0,) * len(shape), pipeline_mode=pl.Buffered(1))
    pair = pl.BlockSpec((2, rows, rows), lambda g: (g, 0, 0))
    hbm = pl.BlockSpec(memory_space=pl.ANY)
    far = [((2, 2, 4, 2 * weight_in.shape[0], 3 * width), bf16), ((2, 2, 4, 2 * weight_in.shape[0], hidden), bf16),
           ((2, 2, 4, 2 * weight_out.shape[0], width), bf16), ((rows, 3 * width), bf16), ((rows, width), bf16), ((rows, width), bf16),
           ((rows, width), f32), ((rows, hidden), bf16), ((rows, hidden), bf16)]
    near = [((vectors.shape[0], width), f32), ((rows, 128), f32), ((rows, width), bf16), ((rows, width), f32),
            ((rows, width), bf16), ((8, width), f32)]
    v = lambda *shape: pltpu.VMEM(shape, bf16)
    vf = lambda *shape: pltpu.VMEM(shape, f32)
    dma = pltpu.SemaphoreType.DMA
    return pl.pallas_call(
        functools.partial(forward_kernel, plan, routes),
        grid=(heads // 2,),
        in_specs=[fixed(weight_in.shape), fixed(weight_out.shape), fixed(vectors.shape), fixed((1, rows)), pair, hbm, hbm],
        out_specs=[pair, pair] + [hbm] * len(far) + [fixed(s) for s, _ in near],
        out_shape=[jax.ShapeDtypeStruct(prev.shape, bf16)] * 2 + [jax.ShapeDtypeStruct(s, t) for s, t in far + near],
        scratch_shapes=[
            vf(2, 2, 4, 32, 128), vf(rows, rows), v(*weight_in.shape), v(*weight_out.shape), vf(16, 128), v(2, width, 768), v(hidden, width),
            v(rows, width), v(rows, width), v(rows, 3 * width), v(rows, width), v(rows, width), vf(rows, width), v(rows, hidden),
            v(2, rows, 768), vf(rows, width), vf(rows, width), dma((11, 10)), dma((11, 10)), dma((8,)), dma((13,))],
        compiler_params=pltpu.CompilerParams(collective_id=1, has_side_effects=True, vmem_limit_bytes=64 * 2**20 - 65536),
        name="forward",
    )(weight_in, weight_out, vectors, seg.reshape(1, rows), prev, tokens, grad_out)


class Scatter:
    def __init__(self, full, got, send_sem, recv_sem):
        self.full, self.got = full, got
        self.send_sem, self.recv_sem = send_sem, recv_sem
        y, c, z, x = self.y, self.c, self.z, self.x = coords()
        first, second = (1 - y) * 2 + c, z * 2 + 1 - x
        self.core = dev(y, 1 - c, z, x)
        self.one = (jnp.where(c == 0, first, y * 2 + c), jnp.where(c == 0, z * 2 + x, second))
        self.two = (jnp.where(c == 0, y * 2 + c, first), jnp.where(c == 0, second, z * 2 + x))
        self.at_one = (jnp.where(c == 0, 1 - y, y), jnp.where(c == 0, x, 1 - x))
        self.at_two = (jnp.where(c == 0, y, 1 - y), jnp.where(c == 0, 1 - x, x))

    def copy(self, src, dst, k, slot, who):
        return pltpu.make_async_remote_copy(
            src_ref=src, dst_ref=dst, send_sem=self.send_sem.at[k, slot], recv_sem=self.recv_sem.at[k, slot],
            device_id=who, device_id_type=MESH)

    def to_core(self, k):
        return self.copy(self.full[k]().at[:, 1 - self.c], self.got[k][0], k, 0, self.core)

    def to_one(self, k):
        full = self.full[k]()
        return [self.copy(full.at[1 - self.y, self.c, :, 1 - self.x], self.got[k][1].at[0], k, 1, self.one),
                self.copy(full.at[self.at_one[0], self.c, :, self.at_one[1]], self.got[k][1].at[1], k, 2, self.one)]

    def to_two(self, k):
        return self.copy(self.full[k]().at[self.at_two[0], self.c, :, self.at_two[1]], self.got[k][2], k, 3, self.two)

    def along_z(self, k):
        full = self.full[k]()
        out = []
        for i in range(3):
            z = lax.rem(self.z + i + 1, 4)
            out.append(self.copy(full.at[self.y, self.c, z, self.x], self.got[k][3].at[i], k, 4 + i, dev(self.y, self.c, z, self.x)))
        return out

    def r1(self, k):
        self.to_core(k).start()

    def r2(self, k):
        full, got = self.full[k](), self.got[k][0]
        self.to_core(k).wait_recv()

        @pl.loop(0, 8)
        def _(i):
            for y in range(2):
                z, x = i // 2, lax.rem(i, 2)
                total = full[y, self.c, z, x].astype(jnp.float32) + got[y, z, x].astype(jnp.float32)
                full[y, self.c, z, x] = total.astype(full.dtype)
        for d in self.to_one(k):
            d.start()

    def r3(self, k):
        full, got = self.full[k](), self.got[k][1]
        for d in self.to_one(k):
            d.wait_recv()
        y, x = self.at_two

        @pl.loop(0, 4)
        def _(z):
            total = full[y, self.c, z, x].astype(jnp.float32) + got[0, z].astype(jnp.float32)
            full[y, self.c, z, x] = total.astype(full.dtype)
        self.to_two(k).start()

    def r4(self, k):
        full = self.full[k]()
        self.to_two(k).wait_recv()

        @pl.loop(0, 4)
        def _(z):
            total = full[self.y, self.c, z, self.x].astype(jnp.float32) + self.got[k][1][1, z].astype(jnp.float32)
            total = total + self.got[k][2][z].astype(jnp.float32)
            full[self.y, self.c, z, self.x] = total.astype(full.dtype)
        for d in self.along_z(k):
            d.start()

    def r5(self, k):
        for d in self.along_z(k):
            d.wait_recv()
        total = self.full[k]()[self.y, self.c, self.z, self.x].astype(jnp.float32)
        for i in range(3):
            total = total + self.got[k][3][i].astype(jnp.float32)
        return total

    def finish(self, k):
        for d in [self.to_core(k), *self.to_one(k), self.to_two(k), *self.along_z(k)]:
            d.wait_send()


def put_rows(ref, start, value):
    size, count = ref.shape[4], value.shape[0]
    for d in range(start // size, (start + count - 1) // size + 1):
        low, high = max(start, d * size), min(start + count, (d + 1) * size)
        ref[d // 16, d // 8 % 2, d // 2 % 4, d % 2, low - d * size:high - d * size] = value[low - start:high - start]


def own_columns(value, shards, columns):
    for d in range(shards):
        at, off = columns * d // 128, columns * d % 128
        if off + columns <= 128:
            tile = value[:, 128 * at:128 * (at + 1)]
            yield d, pltpu.roll(tile, 128 - off, 1) if off else tile
        else:
            yield d, pltpu.roll(value[:, 128 * at:128 * (at + 2)], 256 - off, 1)[:, :128]


def backward_kernel(heads, plan, columns, *refs):
    (ddown_ref, hlow_ref, small_ref, two_ref, sone_ref, probs_ref, dl_ref,
     act_hbm, gp_hbm, go_hbm, gu_hbm, gq_hbm, dsec_hbm, none_hbm, mixed_hbm, x_hbm, qkv_hbm,
     dprev_ref, dx_ref, gin_ref, gout_ref, gvec_ref, norm_ref) = refs[:23]
    qkv_ref, do_ref, x_ref, mixed_ref, act_ref, gp_ref, dup_ref, w_ref, acc_ref, none_ref, part_ref, fvec_ref = refs[23:35]
    ups, outs = refs[35:37]
    got_flat = refs[37:93]
    nmine, ngot, send_sem, recv_sem, loc_sem, ns_sem, nr_sem = refs[93:]
    g = pl.program_id(0)
    rows, width = ddown_ref.shape
    hidden = act_hbm.shape[1]
    tile = 256
    U, O, Q, V = 0, 4, 7, 13
    got = [got_flat[4 * k:4 * k + 4] for k in range(14)]
    full = [lambda k=k: ups.at[k] for k in range(4)] + [lambda j=j: outs.at[j] for j in range(3)]
    full += [lambda p=p: ups.at[p // 2, :, :, :, :, :, :, pl.ds(384 * (p % 2), 384)] for p in range(6)] + [lambda: fvec_ref]
    sc = Scatter(full, got, send_sem, recv_sem)
    y, c, z, x = coords()
    peers = peers_of(y, c, z, x)
    stages = {1: sc.r1, 2: sc.r2, 3: sc.r3, 4: sc.r4}

    def run(place):
        for stage, k in plan.get(place, ()):
            if stage == 5:
                finish(k)
            else:
                stages[stage](k)

    def finish(k):
        total = sc.r5(k)
        if k < O:
            gin_ref[:, :, 3 * width + 768 * k:3 * width + 768 * (k + 1)] = total
        elif k < Q:
            gout_ref[:, :, 256 * (k - O):256 * (k - O + 1)] = total
        elif k < V:
            for i in range(3):
                gin_ref[:, :, width * i + 128 * (k - Q):width * i + 128 * (k - Q + 1)] = total[:, :, 128 * i:128 * (i + 1)]
        else:
            lane = lax.broadcasted_iota(jnp.int32, total.shape, 1)
            gvec_ref[...] = jnp.where(lane < columns, total, 0.0)

    def load(src, dst, i):
        return pltpu.make_async_copy(src, dst, loc_sem.at[i])

    near = [dev(lax.rem(y + i // 4, 2), lax.rem(c + i // 2 % 2, 2), z, lax.rem(x + i % 2, 2)) for i in range(1, 8)]
    far = [dev(y, c, lax.rem(z + i, 4), x) for i in (1, 2, 3)]

    def share(i):
        return pltpu.make_async_remote_copy(
            src_ref=nmine.at[0 if i < 7 else 1], dst_ref=ngot.at[i], send_sem=ns_sem.at[i], recv_sem=nr_sem.at[i],
            device_id=(near + far)[i], device_id_type=MESH)

    def in_order(values, index):
        total = jnp.zeros_like(values[0])
        for at in range(len(values)):
            for i, v in enumerate(values):
                total = total + jnp.where(index(i) == at, v, 0.0)
        return total

    w_out, w_up, w_qkv = go_hbm.reshape(width + hidden, width), gu_hbm.reshape(width, hidden), gq_hbm.reshape(width, 3 * width)
    late = lambda: [load(dsec_hbm, acc_ref, 0), load(none_hbm, none_ref, 1), load(mixed_hbm, mixed_ref, 2), load(x_hbm, x_ref, 3),
                    load(qkv_hbm, qkv_ref, 4), load(act_hbm, act_ref, 8)]
    last_w = lambda: [load(w_qkv.at[:, pl.ds(768 * i, 768)], w_ref.at[i], 5 + i) for i in range(3)]

    @pl.when(g == 0)
    def _():
        barrier = pltpu.get_barrier_semaphore()
        met = far + near
        for p in met:
            pl.semaphore_signal(barrier, inc=1, device_id=p, device_id_type=MESH)

        def ahead(k):
            return [load(w_out.at[pl.ds(width + 768 * k, 768), :], w_ref.at[0], 5), load(gp_hbm.at[:, pl.ds(768 * k, 768)], gp_ref, 6)]

        def behind(k):
            return [load(w_up.at[:, pl.ds(768 * k, 768)], w_ref.at[1], 7)]
        for d in ahead(0) + behind(0) + late():
            d.start()
        part_ref[...] = jnp.zeros_like(part_ref)
        part_ref[1:2, :] = two_ref[0:1, :]
        part_ref[3:4, :] = two_ref[1:2, :]
        part_ref[7:8, :] = two_ref[2:3, :]
        pl.semaphore_wait(barrier, len(met))

        @pl.loop(0, 4)
        def _(k):
            for i in range(4):
                @pl.when(k == i)
                def _():
                    for d in ahead(i):
                        d.wait()
            low = (dotf(ddown_ref[...], w_ref[0], NT) * gp_ref[...].astype(jnp.float32)).astype(jnp.bfloat16)
            dup_ref[...] = low
            part_ref[pl.ds(8 + k, 1), :] = jnp.sum(low.astype(jnp.float32), axis=0, keepdims=True)
            ups[k] = dotf(hlow_ref[...], dup_ref[...], TN).reshape(ups.shape[1:]).astype(jnp.bfloat16)
            for i in range(4):
                @pl.when(k == i)
                def _():
                    sc.r1(U + i)
                    if i < 3:
                        for d in ahead(i + 1):
                            d.start()
                    run(("down", i))
                    if i == 0:
                        late()[0].wait()
                    for d in behind(i):
                        d.wait()
            acc_ref[...] += dotf(dup_ref[...], w_ref[1], NT)
            for i in range(4):
                @pl.when(k == i)
                def _():
                    if i < 3:
                        for d in behind(i + 1):
                            d.start()
                    run(("up", i))

        wo = load(w_out.at[pl.ds(0, width), :], w_ref.at[0], 5)
        wo.start()
        late()[1].wait()

        @pl.loop(0, rows // 128)
        def _(i):
            sl = pl.ds(pl.multiple_of(i * 128, 128), 128)
            one, normed = acc_ref[sl, :], none_ref[sl, :]
            part_ref[0:1, :] += jnp.sum(one * normed, axis=0, keepdims=True)
            part_ref[2:3, :] += jnp.sum(one, axis=0, keepdims=True)
            back = norm_back(one, normed, sone_ref[sl, 0:1], small_ref[0:1, :])
            low = back.astype(jnp.bfloat16)
            acc_ref[sl, :] = back
            dup_ref[sl, :] = low
            part_ref[6:7, :] += jnp.sum(low.astype(jnp.float32), axis=0, keepdims=True)
        run("norm")
        late()[2].wait()
        late()[5].wait()

        def put(start, value):
            for j in range(3):
                put_rows(outs.at[j], start, value[:, tile * j:tile * (j + 1)].reshape(96, 8, tile).astype(jnp.bfloat16))
        put(0, dotf(mixed_ref[...], dup_ref[...], TN))
        for k in range(4):
            put((width + 768 * k) // 8, dotf(act_ref[:, 768 * k:768 * (k + 1)], ddown_ref[...], TN))
        for j in range(3):
            sc.r1(O + j)
        run("out")
        wo.wait()
        do_ref[...] = dotf(dup_ref[...], w_ref[0], NT).astype(jnp.bfloat16)
        for d in late()[3:5]:
            d.wait()
        for d in last_w():
            d.start()

    for i in range(heads):
        if plan.get(("head", i)):
            @pl.when(g == i)
            def _():
                run(("head", i))

    pair, half = g // 2, lax.rem(g, 2)
    at = lambda off: pl.ds(pl.multiple_of(off * width + pair * 128, 128), 128)
    lane = lax.broadcasted_iota(jnp.int32, (rows, 128), 1)
    pick = lambda v: jnp.where(lane // 64 == half, v, jnp.zeros_like(v))
    q2, k2, v2, do2 = qkv_ref[:, at(0)], qkv_ref[:, at(1)], qkv_ref[:, at(2)], do_ref[:, at(0)]
    p = probs_ref[0].astype(jnp.float32)
    dp = dotf(pick(do2), v2, NT)
    ds = p * (dp - jnp.sum(p * dp, axis=1, keepdims=True))
    grad = (ds + dl_ref[0].astype(jnp.float32)).astype(jnp.bfloat16)
    dprev_ref[0] = grad
    dq = (dotf(grad, pick(k2), NN) * 0.125).astype(jnp.bfloat16)
    dk = (dotf(dprev_ref[0], pick(q2), TN) * 0.125).astype(jnp.bfloat16)
    dv = dotf(probs_ref[0], pick(do2), TN).astype(jnp.bfloat16)

    @pl.when(half == 0)
    def _():
        for i, v in enumerate((dq, dk, dv)):
            gp_ref[:, 128 * i:128 * (i + 1)] = v

    @pl.when(half == 1)
    def _():
        for i, v in enumerate((dq, dk, dv)):
            v = gp_ref[:, 128 * i:128 * (i + 1)] + v
            gp_ref[:, 128 * i:128 * (i + 1)] = v
            qkv_ref[:, at(i)] = v
            if i != 1:
                part_ref[4 + i // 2:5 + i // 2, at(0)] = jnp.sum(v.astype(jnp.float32), axis=0, keepdims=True)
        for p in range(0, heads // 2, 2):
            @pl.when(pair == p)
            def _():
                sc.finish(U + p // 2)
        to = pl.ds(pl.multiple_of(384 * lax.rem(pair, 2), 384), 384)
        ups[pair // 2, :, :, :, :, :, :, to] = dotf(x_ref[...], gp_ref[:, 0:384], TN).reshape(ups.shape[1:7] + (384,)).astype(jnp.bfloat16)
        for p in range(heads // 2):
            @pl.when(pair == p)
            def _():
                sc.r1(Q + p)

    @pl.when(g == heads - 1)
    def _():
        for d, tile_of in own_columns(part_ref[...], 32, columns):
            fvec_ref[d // 16, d // 8 % 2, d // 2 % 4, d % 2] = tile_of
        sc.r1(V)
        run("end")
        for d in last_w():
            d.wait()

        @pl.loop(0, 3)
        def _(i):
            acc_ref[...] += dotf(qkv_ref[:, pl.ds(pl.multiple_of(768 * i, 768), 768)], w_ref[i], NT)
            for j in range(3):
                @pl.when(i == j)
                def _():
                    run(("dx", j))
        dx_ref[...] = acc_ref[...].astype(jnp.bfloat16)
        run("last")
        squares = gvec_ref[0:8, :] * gvec_ref[0:8, :] + gvec_ref[8:16, :] * gvec_ref[8:16, :]
        for ref in (gin_ref, gout_ref):
            v = ref[...]
            v = jnp.sum(v * v, axis=0)
            for j in range(v.shape[1] // 128):
                squares = squares + v[:, 128 * j:128 * (j + 1)]
        nmine[0] = jnp.sum(squares, keepdims=True) + jnp.zeros((8, 128), jnp.float32)
        for i in range(7):
            share(i).start()
        for k in range(14):
            if k not in (0, 1, 2):
                sc.finish(k)
        for i in range(7):
            share(i).wait_recv()
        me = y * 4 + c * 2 + x

        def from_near(i):
            return me if i == 0 else lax.rem(y + i // 4, 2) * 4 + lax.rem(c + i // 2 % 2, 2) * 2 + lax.rem(x + i % 2, 2)
        plane = in_order([nmine[0]] + [ngot[i] for i in range(7)], from_near)
        nmine[1] = plane
        for i in range(7, 10):
            share(i).start()
        for i in range(7, 10):
            share(i).wait_recv()
        total = in_order([plane] + [ngot[i] for i in range(7, 10)], lambda i: lax.rem(z - i + 4, 4))
        norm_ref[...] = jnp.sqrt(total)
        for i in range(10):
            share(i).wait_send()


def backward_all(plan, columns, grad_down, hidden_low, small, two_sums, scale_one, probs, grad_logits,
                 activated, slope, full_out, full_up, full_qkv, grad_second, normed_one, mixed, tokens, qkv):
    rows, width = tokens.shape
    heads = probs.shape[0]
    hidden = activated.shape[1]
    f32, bf16 = jnp.float32, jnp.bfloat16
    fixed = lambda shape: pl.BlockSpec(shape, lambda g: (0,) * len(shape), pipeline_mode=pl.Buffered(1))
    head = pl.BlockSpec((1, rows, rows), lambda g: (g, 0, 0))
    hbm = pl.BlockSpec(memory_space=pl.ANY)
    r_in, r_out = full_qkv.shape[3] // 2, full_out.shape[3] // 2
    landing = []
    for r, n in [(r_in, 768)] * 4 + [(r_out, 256)] * 3 + [(r_in, 384)] * 6:
        landing += [pltpu.VMEM(lead + (r // 8, 8, n), bf16) for lead in ((2, 4, 2), (2, 4), (4,), (3,))]
    landing += [pltpu.VMEM(lead + (16, 128), f32) for lead in ((2, 4, 2), (2, 4), (4,), (3,))]
    lead = (2, 2, 4, 2)
    v = lambda *shape: pltpu.VMEM(shape, bf16)
    vf = lambda *shape: pltpu.VMEM(shape, f32)
    shapes = [((r_in // 8, 8, 3 * width + hidden), f32), ((r_out // 8, 8, width), f32), ((16, 128), f32), ((8, 128), f32)]
    dma = pltpu.SemaphoreType.DMA
    return pl.pallas_call(
        functools.partial(backward_kernel, heads, plan, columns),
        grid=(heads,),
        in_specs=[fixed((rows, width)), fixed((rows, width)), fixed(small.shape), fixed(two_sums.shape),
                  fixed(scale_one.shape), head, head] + [hbm] * 10,
        out_specs=[head, fixed((rows, width))] + [fixed(s) for s, _ in shapes],
        out_shape=[jax.ShapeDtypeStruct(probs.shape, bf16), jax.ShapeDtypeStruct((rows, width), bf16)]
        + [jax.ShapeDtypeStruct(s, t) for s, t in shapes],
        scratch_shapes=[v(rows, 3 * width), v(rows, width), v(rows, width), v(rows, width), v(rows, hidden),
                        v(rows, 768), v(rows, 768), v(3, 768, width), vf(rows, width), vf(rows, width),
                        vf(16, width), vf(*lead, 16, 128)]
        + [v(4, *lead, r_in // 8, 8, 768), v(3, *lead, r_out // 8, 8, 256)] + landing
        + [vf(2, 8, 128), vf(10, 8, 128), dma((14, 7)), dma((14, 7)), dma((10,)), dma((10,)), dma((10,))],
        compiler_params=pltpu.CompilerParams(collective_id=2, has_side_effects=True, vmem_limit_bytes=64 * 2**20 - 65536),
        name="backward",
    )(grad_down, hidden_low, small, two_sums, scale_one, probs, grad_logits,
      activated, slope, full_out, full_up, full_qkv, grad_second, normed_one, mixed, tokens, qkv)


def update_kernel(norm_ref, step_ref, *refs):
    through, refs = refs[:4], refs[4:]
    trios, refs = [refs[4 * i:4 * i + 4] for i in range(3)], refs[12:]
    through_out, refs = refs[:4], refs[4:]
    outs, gn_ref = [refs[5 * i:5 * i + 5] for i in range(3)], refs[15]
    for a, b in zip(through, through_out):
        b[...] = a[...]
    norm = norm_ref[0:1, 0:1]
    gn_ref[...] = norm
    factor = jnp.minimum(1.0, clip_scale * math.sqrt(PARAMS) / (norm + 1e-06))
    step = jnp.full((1, 1), step_ref[0], jnp.int32).astype(jnp.float32)
    one = 1.0 - jnp.exp(step * math.log(beta_one))
    two = 1.0 - jnp.exp(step * math.log(beta_two))
    for i, ((g_ref, w_ref, m_ref, v_ref), out) in enumerate(zip(trios, outs)):
        rate, decay = (rate_vector, 0.0) if i == 2 else (rate_matrix, decay_matrix)
        grad = g_ref[...].reshape(w_ref.shape) if i < 2 else g_ref[0:w_ref.shape[0], 0:w_ref.shape[1]]
        clipped = grad * factor
        moment = beta_one * m_ref[...] + (1.0 - beta_one) * clipped
        square = beta_two * v_ref[...] + (1.0 - beta_two) * clipped * clipped
        weight = w_ref[...] - rate * ((moment / one) / (jnp.sqrt(square / two) + adam_eps) + decay * w_ref[...])
        for ref, val in zip(out, (clipped, moment, square, weight, weight.astype(jnp.bfloat16))):
            ref[...] = val


def update_all(norm, step_count, through, trios):
    steps = 6
    f32 = jnp.float32

    def spec(a):
        if a.shape[-1] < 128 * steps:
            return pl.BlockSpec(a.shape, lambda g: (0,) * a.ndim)
        return pl.BlockSpec(a.shape[:-1] + (a.shape[-1] // steps,), lambda g: (0,) * (a.ndim - 1) + (g,))
    slabs = [pl.BlockSpec((a.shape[0] // steps,) + a.shape[1:], lambda g: (g, 0, 0)) if a.ndim == 3 else spec(a) for a in through]
    shapes = []
    for g, w, m, v in trios:
        shapes += [jax.ShapeDtypeStruct(w.shape, t) for t in (f32, f32, f32, f32, jnp.bfloat16)]
    flat = [a for trio in trios for a in trio]
    return pl.pallas_call(
        update_kernel,
        grid=(steps,),
        in_specs=[pl.BlockSpec((8, 128), lambda g: (0, 0)), pl.BlockSpec(memory_space=pltpu.SMEM)] + slabs + [spec(a) for a in flat],
        out_specs=slabs + [spec(s) for s in shapes] + [pl.BlockSpec((1, 1), lambda g: (0, 0))],
        out_shape=[jax.ShapeDtypeStruct(a.shape, a.dtype) for a in through] + shapes + [jax.ShapeDtypeStruct((1, 1), f32)],
        compiler_params=pltpu.CompilerParams(vmem_limit_bytes=64 * 2**20 - 65536),
        name="update",
    )(norm, step_count, *through, *flat)


def adam_update(master, moment, square, gradient, factor, step_value, step_rate, decay_rate):
    clipped = gradient * factor
    new_moment = beta_one * moment + (1.0 - beta_one) * clipped
    new_square = beta_two * square + (1.0 - beta_two) * clipped * clipped
    fixed_moment = new_moment / (1.0 - jnp.power(beta_one, step_value))
    fixed_square = new_square / (1.0 - jnp.power(beta_two, step_value))
    updated = master - step_rate * (
        fixed_moment / (jnp.sqrt(fixed_square) + adam_eps) + decay_rate * master
    )
    return (clipped, new_moment, new_square, updated)


def rounded(v):
    return lax.reduce_precision(v, 8, 7)


def gather_all(weight_in, weight_out, vectors, width):
    whole = lambda v: lax.all_gather(v, AXES, axis=0, tiled=True)
    low_in = weight_in.astype(jnp.bfloat16)
    small = lax.all_gather(rounded(vectors), AXES, axis=1, tiled=True)
    return whole(low_in[:, : 3 * width]), whole(low_in[:, 3 * width :]), whole(weight_out.astype(jnp.bfloat16)), small


def forward_plain(tokens, grad_out, full_qkv, full_up, full_out, small, prev, segments):
    width = tokens.shape[1]
    dot = lambda a, b: jnp.dot(a, b, preferred_element_type=jnp.float32)
    sums = lambda v: jnp.sum(v, axis=0, dtype=jnp.float32)
    offsets = jnp.concatenate([small[4], jnp.zeros_like(small[4]), small[5]])
    qkv = (dot(tokens, full_qkv) + offsets).astype(jnp.bfloat16)
    logits, mixed, log_sums = attn_fwd(qkv, prev, segments, 640)
    first = tokens.astype(jnp.float32) + (dot(mixed, full_out[:width]) + small[6])
    hidden_one, normed_one, scale_one = norm_rows(first, small[0], small[2])
    hidden_low = hidden_one.astype(jnp.bfloat16)
    upward = dot(hidden_low, full_up) + small[8:].reshape(-1)
    activated, gelu_pull = jax.vjp(gelu_exact, upward)
    activated, slope = activated.astype(jnp.bfloat16), gelu_pull(jnp.ones_like(upward))[0]
    second = hidden_one + (dot(activated, full_out[width:]) + small[7])
    output, normed_two, scale_two = norm_rows(second, small[1], small[3])
    grad_output = grad_out.astype(jnp.float32)
    grad_second = norm_back(grad_output, normed_two, scale_two, small[1])
    grad_down = grad_second.astype(jnp.bfloat16)
    two_sums = jnp.stack([sums(grad_output * normed_two), sums(grad_output), sums(grad_down)])
    return (logits, qkv, mixed, log_sums, hidden_low, normed_one, scale_one, activated, slope, output.astype(jnp.bfloat16),
            grad_second, grad_down, two_sums)


def reduce_all(grad_qkv, grad_up, grad_out, small, shards):
    part = lambda v: lax.psum_scatter(v, AXES, scatter_dimension=0, tiled=True).astype(jnp.float32)
    owned_in = jnp.concatenate([part(grad_qkv), part(grad_up)], axis=1)
    owned_out = part(grad_out)
    owned_small = lax.psum_scatter(small, AXES, scatter_dimension=1, tiled=True)
    total = lax.psum(jnp.sum(owned_in**2) + jnp.sum(owned_out**2) + jnp.sum(owned_small**2), AXES)
    return owned_in, owned_out, owned_small, jnp.sqrt(total)


def body(remote, hidden_in, prev_logits, segment_ids, d_hidden, d_logits, weight_in, weight_out, vectors,
         moment_in, moment_out, moment_vectors, square_in, square_out, square_vectors, step_count):
    width = weight_out.shape[1]
    shards = lax.axis_size("dp") * lax.axis_size("fsdp")
    dot = lambda spec, a, b: jnp.einsum(spec, a, b, preferred_element_type=jnp.float32)
    sums = lambda v: jnp.sum(v, axis=0, dtype=jnp.float32)
    segments = segment_ids[0]
    if remote:
        (logits, probs, full_qkv, full_up, full_out, qkv, mixed, hidden_low, normed_one, activated, slope, small, scale_one,
         output, grad_second, grad_down, two_sums) = forward_all(
             FORWARD_PLAN, ROUTES, hidden_in, d_hidden, weight_in, weight_out, vectors, prev_logits[0], segments)
        grad_prev, grad_tokens, grad_in, grad_out, grad_vec, norm = backward_all(
            BACKWARD_PLAN, vectors.shape[1], grad_down, hidden_low, small, two_sums, scale_one, probs, d_logits[0],
            activated, slope, full_out, full_up, full_qkv, grad_second, normed_one, mixed, hidden_in, qkv)
        (logits, grad_prev, output, grad_tokens, *states, grad_norm) = update_all(
            norm, step_count, [logits, grad_prev, output, grad_tokens],
            [(grad_in, weight_in, moment_in, square_in), (grad_out, weight_out, moment_out, square_out),
             (grad_vec, vectors, moment_vectors, square_vectors)])
        clipped, moments, squares, updated, copies = [states[i::5] for i in range(5)]
        return (output, logits[None], grad_tokens, grad_prev[None], *clipped, *moments, *squares, *updated, *copies, grad_norm[0, 0])
    (full_qkv, full_up, full_out, small) = gather_all(weight_in, weight_out, vectors, width)
    (logits, qkv, mixed, log_sums, hidden_low, normed_one, scale_one, activated, slope, output,
     grad_second, grad_down, two_sums) = forward_plain(hidden_in, d_hidden, full_qkv, full_up, full_out, small, prev_logits[0], segments)
    w_attn, w_down = full_out[:width], full_out[width:]
    down_grad = dot("tf,td->fd", activated, grad_down).astype(jnp.bfloat16)
    grad_up = (dot("td,fd->tf", grad_down, w_down) * slope).astype(jnp.bfloat16)
    up_grad = dot("td,tf->df", hidden_low, grad_up).astype(jnp.bfloat16)
    grad_one = grad_second + dot("tf,df->td", grad_up, full_up)
    grad_first = norm_back(grad_one, normed_one, scale_one, small[0])
    grad_attn = grad_first.astype(jnp.bfloat16)
    attn_grad = dot("tc,td->cd", mixed, grad_attn).astype(jnp.bfloat16)
    grad_mixed = dot("td,cd->tc", grad_attn, w_attn).astype(jnp.bfloat16)
    grad_prev, grad_q, grad_k, grad_v = attn_bwd(qkv, grad_mixed, prev_logits[0], d_logits[0], log_sums, segments, 640)
    grad_qkv = jnp.concatenate([grad_q, grad_k, grad_v], axis=1)
    qkv_grad = dot("td,tc->dc", hidden_in, grad_qkv).astype(jnp.bfloat16)
    grad_tokens = (grad_first + dot("tc,dc->td", grad_qkv, full_qkv)).astype(jnp.bfloat16)
    small_grad = jnp.concatenate([
        jnp.stack([sums(grad_one * normed_one), two_sums[0], sums(grad_one), two_sums[1],
                   sums(grad_q), sums(grad_v), sums(grad_attn), two_sums[2]]),
        sums(grad_up).reshape(-1, width)], axis=0)

    owned_in, owned_out, owned_small, grad_norm = reduce_all(
        qkv_grad, up_grad, jnp.concatenate([attn_grad, down_grad], axis=0), small_grad, shards)
    factor = jnp.minimum(1.0, clip_scale * math.sqrt(PARAMS) / (grad_norm + 1e-06))
    step_value = step_count[0].astype(jnp.float32)
    new = [
        adam_update(weight_in, moment_in, square_in, owned_in, factor, step_value, rate_matrix, decay_matrix),
        adam_update(weight_out, moment_out, square_out, owned_out, factor, step_value, rate_matrix, decay_matrix),
        adam_update(vectors, moment_vectors, square_vectors, owned_small, factor, step_value, rate_vector, 0.0),
    ]
    clipped, moments, squares, updated = zip(*new)
    return (output.astype(jnp.bfloat16), logits[None], grad_tokens, grad_prev[None],
            *clipped, *moments, *squares, *updated, *[u.astype(jnp.bfloat16) for u in updated], grad_norm)


def solution(mesh):
    remote = (mesh.shape["dp"], mesh.shape["fsdp"]) == (4, 8)
    rows = P(AXES, None)
    heads = P(AXES, None, None, None)
    cols = P(None, AXES)
    trio = (rows, rows, cols)
    return jax.shard_map(
        functools.partial(body, remote),
        mesh=mesh,
        in_specs=(rows, heads, rows, rows, heads, *trio, *trio, *trio, P()),
        out_specs=(rows, heads, rows, heads, *trio, *trio, *trio, *trio, *trio, P()),
        check_vma=False,
    )
```

profile of v0, /device:TPU:0, one launch (start us, length us, event | category | flops | bytes accessed | tf_op | source)
XLA Modules:
  0.0 216.2 jit_solution(744386063583259693)
XLA Ops:
  0.7 93.0 %forward.1 = (bf16[12,640,640]{2,1,0:T(8,128)(2,1)}, bf16[12,640,640]{2,1,0:T(8,128)(2,1)}, bf16[2,2,4,48,2304]{4,3,2,1,0:T(8,128)(2,1)}, bf16[2,2,4,48,3072]{4,...) custom-call(f32[24,5376]{1,0:T(8,128)} %refs_5_.1, ...), custom_call_target="tpu_custom_call" | custom-call | tf_op jit(solution)/shard_map/forward/pallas_call | solution.py:596
  93.6 104.5 %backward.1 = (bf16[12,640,640]{2,1,0:T(8,128)(2,1)}, bf16[640,768]{1,0:T(8,128)(2,1)}, f32[3,8,5376]{2,1,0:T(8,128)}, f32[15,8,768]{2,1,0:T(8,128)}, f32[16,128]{1,0:T(8,128)}, /*index=5*/f32[8,128]{1,0:T(8,128)}) custom-call(bf16[640,768]{1,0:T(8,128)(2,1)} %get-tuple-element.63.refs_0_, bf16[640,768]{1,0:T(8,128)(2,1)} %get-tuple-element.64.refs_1_, ...), custom_call_target="tpu_custom_call" | custom-call | tf_op jit(solution)/shard_map/backward/pallas_call | solution.py:979
  198.8 17.3 %update.1 = (bf16[12,640,640]{2,1,0:T(8,128)(2,1)}, bf16[12,640,640]{2,1,0:T(8,128)(2,1)}, bf16[640,768]{1,0:T(8,128)(2,1)}, bf16[640,768]{1,0:T(8,128)(2,1)}, f...) custom-call(f32[8,128]{1,0:T(8,128)} %get-tuple-element.78.norm_ref,, ...), custom_call_target="tpu_custom_call" | custom-call | tf_op jit(solution)/shard_map/update/pallas_call | solution.py:1035
where the time goes:
time: 217 us; the launch traced here: 216 us
  Pallas kernels  215 us (99%)
    pallas_call x1, Pallas kernels, backward_all(): pl.pallas_call(functools.partial(backward_kernel, heads, plan, columns),...  105 us
    pallas_call x1, Pallas kernels, forward_all(): pl.pallas_call(functools.partial(forward_kernel, plan, routes), grid=(hea...  93 us
    pallas_call x1, Pallas kernels, update_all(): pl.pallas_call(update_kernel, grid=(steps,), in_specs=[pl.BlockSpec((8, 1...  17.3 us

commit v1 on v0

--- a/solution.py
+++ b/solution.py
@@ -212,6 +212,7 @@
 
 
 ROUTES = "zzzzzzznnnn"
+BACKWARD_ROUTES = "nzzznzzzzznzzz"
 FORWARD_PLAN = {
     "start": [(1, 7), (1, 8), (1, 9), (1, 10), (1, 0), (2, 0), (1, 1), (3, 0)],
     ("q", 0): [(1, 2), (2, 1), (1, 3), (2, 2), (3, 1)],
@@ -228,25 +229,25 @@
     ("up", 2): [(3, 10)],
 }
 BACKWARD_PLAN = {
-    ("up", 1): [(2, 0)],
+    ("down", 1): [(2, 0)],
     ("down", 2): [(2, 1)],
     ("down", 3): [(3, 0), (2, 2)],
-    "norm": [(3, 1), (4, 0), (2, 3)],
-    "out": [(4, 1), (3, 2)],
-    ("head", 0): [(3, 3), (5, 0)],
-    ("head", 2): [(4, 2), (4, 3), (2, 4), (2, 5), (5, 1)],
-    ("head", 3): [(2, 6), (2, 7)],
-    ("head", 4): [(5, 2)],
-    ("head", 5): [(3, 4)],
-    ("head", 6): [(2, 8), (5, 3)],
-    ("head", 7): [(3, 5)],
-    ("head", 8): [(2, 9)],
-    ("head", 9): [(3, 6)],
-    ("head", 10): [(3, 7), (2, 10), (4, 4)],
-    ("head", 11): [(3, 8), (2, 11)],
-    "end": [(4, 5), (3, 9)],
-    ("dx", 1): [(4, 6), (4, 7), (2, 12), (2, 13), (3, 10), (5, 4)],
-    "last": [(4, 8), (4, 9), (3, 11), (3, 12), (5, 5), (3, 13), (4, 10), (4, 11), (4, 12), (4, 13), (5, 6), (5, 7), (5, 8), (5, 9), (5, 10), (5, 11), (5, 12), (5, 13)],
+    ("up", 3): [(3, 1)],
+    "norm": [(2, 3)],
+    "out": [(4, 0), (4, 1), (3, 2), (3, 3)],
+    ("head", 1): [(5, 0), (2, 4), (4, 2)],
+    ("head", 2): [(4, 3), (5, 1), (2, 5)],
+    ("head", 4): [(3, 4), (2, 6), (5, 2)],
+    ("head", 5): [(5, 3)],
+    ("head", 6): [(3, 5)],
+    ("head", 8): [(3, 6)],
+    ("head", 9): [(4, 5), (2, 7), (2, 8)],
+    ("head", 10): [(4, 4), (4, 6), (2, 9), (3, 7)],
+    ("head", 11): [(3, 8), (2, 10), (5, 4), (2, 11)],
+    "end": [(4, 7), (4, 8), (3, 9), (5, 5), (3, 10)],
+    ("dx", 0): [(2, 12), (3, 11)],
+    ("dx", 1): [(4, 9), (2, 13), (5, 6)],
+    "last": [(5, 7), (3, 12), (5, 8), (4, 11), (3, 13), (4, 12), (4, 10), (4, 13), (5, 9), (5, 10), (5, 11), (5, 12), (5, 13)],
 }
 
 
@@ -388,10 +389,10 @@
 
 
 def forward_kernel(plan, routes, win_ref, wout_ref, vec_ref, srow_ref, prev_ref, x_hbm, dout_hbm,
-                   logits_ref, probs_ref, gq_ref, gu_ref, go_ref, qkv_hbm, mixed_hbm, hlow_hbm, none_hbm, act_hbm, gp_hbm,
-                   small_ref, sone_ref, out_ref, dsec_ref, ddown_ref, sums_ref,
+                   logits_ref, probs_ref, gq_ref, gu_ref, go_ref, qkv_hbm, mixed_hbm, hlow_hbm, none_hbm, act_hbm, gp_hbm, out_hbm, dsec_hbm, ddown_hbm,
+                   small_ref, sone_ref, sums_ref,
                    gv_ref, mask_ref, cin_ref, cout_ref, cvec_ref, w_ref, wo_ref, x_ref, dout_ref, qkv_ref, mixed_ref, hlow_ref, none_ref,
-                   act_ref, gp_ref, hid_ref, sec_ref, send_sem, recv_sem, loc_sem, out_sem):
+                   act_ref, gp_ref, hid_ref, sec_ref, out_ref, dsec_ref, ddown_ref, send_sem, recv_sem, loc_sem, out_sem, row_sem):
     g = pl.program_id(0)
     rows, width = x_hbm.shape
     hidden = act_hbm.shape[1]
@@ -418,9 +419,13 @@
                       load(cout_ref, go_ref.at[y, c, z, ga.rows_of(O, x)], 2)]
     x_in, dout_in = lambda: load(x_hbm, x_ref, 3), lambda: load(dout_hbm, dout_ref, 4)
     w_out, w_up, w_qkv = go_ref.reshape(width + hidden, width), gu_ref.reshape(width, hidden), gq_ref.reshape(width, 3 * width)
-    w_q = lambda k: load(w_qkv.at[:, pl.ds(768 * k, 768)], w_ref.at[k % 2], 5 + k % 2)
-    w_u = lambda k: load(w_up.at[:, pl.ds(768 * k, 768)], w_ref.at[(k + 1) % 2], 5 + (k + 1) % 2)
-    w_o = lambda: load(w_out.at[pl.ds(0, width), :], w_ref.at[0], 5)
+
+    def quarters(src, columns, slot):
+        size = width // 4
+        return [load(src.at[pl.ds(size * i, size), columns], w_ref.at[slot, pl.ds(size * i, size), :], 8 + 4 * slot + i) for i in range(4)]
+    w_q = lambda k: quarters(w_qkv, pl.ds(768 * k, 768), k % 2)
+    w_u = lambda k: quarters(w_up, pl.ds(768 * k, 768), (k + 1) % 2)
+    w_o = lambda: quarters(w_out, slice(None), 0)
     w_down = lambda: load(w_out.at[pl.ds(width, hidden), :], wo_ref, 7)
     saves = {"mixed": lambda: save(mixed_ref, mixed_hbm, 1), "hlow": lambda: save(hlow_ref, hlow_hbm, 2),
              "none": lambda: save(none_ref, none_hbm, 3), "qkv": lambda: save(qkv_ref, qkv_hbm, 4)}
@@ -465,9 +470,11 @@
                 def _():
                     run(("q", i))
                     ga.s4(Q + i)
-                    w_q(i).start()
+                    for d in w_q(i):
+                        d.start()
                     run(("qw", i))
-                    w_q(i).wait()
+                    for d in w_q(i):
+                        d.wait()
             bias = jnp.where(k == 1, 0.0, small_ref[pl.ds(4 + k // 2, 1), :])
             v = dotf(x_ref[...], w_ref[lax.rem(k, 2)], NN) + bias
             qkv_ref[:, pl.ds(pl.multiple_of(768 * k, 768), 768)] = v.astype(jnp.bfloat16)
@@ -503,10 +510,12 @@
         run("out")
         for k in range(3):
             ga.s4(O + k)
-        w_o().start()
+        for d in w_o():
+            d.start()
         w_down().start()
         run("outw")
-        w_o().wait()
+        for d in w_o():
+            d.wait()
         hid_ref[...] = x_ref[...].astype(jnp.float32) + (dotf(mixed_ref[...], w_ref[0], NN) + small_ref[6:7, :])
         run("norm")
 
@@ -517,7 +526,7 @@
             none_ref[sl, :] = normed
             sone_ref[sl, :] = jnp.broadcast_to(scaling, (128, 128))
             hid = normed * small_ref[0:1, :] + small_ref[2:3, :]
-            hid_ref[sl, :] = hid
+            sec_ref[sl, :] = hid + small_ref[7:8, :]
             hlow_ref[sl, :] = hid.astype(jnp.bfloat16)
 
         saves["none"]().start()
@@ -530,9 +539,11 @@
                 def _():
                     run(("up", i))
                     ga.s4(U + i)
-                    w_u(i).start()
+                    for d in w_u(i):
+                        d.start()
                     run(("upw", i))
-                    w_u(i).wait()
+                    for d in w_u(i):
+                        d.wait()
                     if i >= 2:
                         save_gp(i - 2).wait()
 
@@ -549,10 +560,17 @@
                 def _():
                     save_act(i).start()
                     save_gp(i).start()
-        w_down().wait()
-        sec_ref[...] = hid_ref[...] + (dotf(act_ref[...], wo_ref[...], NN) + small_ref[7:8, :])
+                    if i == 0:
+                        w_down().wait()
+            part = pl.ds(pl.multiple_of(768 * k, 768), 768)
+            sec_ref[...] += dotf(act_ref[:, part], wo_ref[part, :], NN)
         sums_ref[...] = jnp.zeros_like(sums_ref)
         dout_in().wait()
+
+        def row_saves(i):
+            sl = pl.ds(pl.multiple_of(i * 128, 128), 128)
+            return [pltpu.make_async_copy(a.at[sl, :], b.at[sl, :], row_sem.at[n, i])
+                    for n, (a, b) in enumerate(((out_ref, out_hbm), (dsec_ref, dsec_hbm), (ddown_ref, ddown_hbm)))]
 
         @pl.loop(0, rows // 128)
         def _(i):
@@ -567,6 +585,8 @@
             sums_ref[0:1, :] += jnp.sum(dy * normed, axis=0, keepdims=True)
             sums_ref[1:2, :] += jnp.sum(dy, axis=0, keepdims=True)
             sums_ref[2:3, :] += jnp.sum(low.astype(jnp.float32), axis=0, keepdims=True)
+            for d in row_saves(i):
+                d.start()
         for k in range(len(chunks)):
             ga.finish(k)
         for s in saves.values():
@@ -575,6 +595,11 @@
             save_act(k).wait()
         for k in (2, 3):
             save_gp(k).wait()
+
+        @pl.loop(0, rows // 128)
+        def _(i):
+            for d in row_saves(i):
+                d.wait()
 
 
 def forward_all(plan, routes, tokens, grad_out, weight_in, weight_out, vectors, prev, seg):
@@ -587,9 +612,8 @@
     hbm = pl.BlockSpec(memory_space=pl.ANY)
     far = [((2, 2, 4, 2 * weight_in.shape[0], 3 * width), bf16), ((2, 2, 4, 2 * weight_in.shape[0], hidden), bf16),
            ((2, 2, 4, 2 * weight_out.shape[0], width), bf16), ((rows, 3 * width), bf16), ((rows, width), bf16), ((rows, width), bf16),
-           ((rows, width), f32), ((rows, hidden), bf16), ((rows, hidden), bf16)]
-    near = [((vectors.shape[0], width), f32), ((rows, 128), f32), ((rows, width), bf16), ((rows, width), f32),
-            ((rows, width), bf16), ((8, width), f32)]
+           ((rows, width), f32), ((rows, hidden), bf16), ((rows, hidden), bf16), ((rows, width), bf16), ((rows, width), f32), ((rows, width), bf16)]
+    near = [((vectors.shape[0], width), f32), ((rows, 128), f32), ((8, width), f32)]
     v = lambda *shape: pltpu.VMEM(shape, bf16)
     vf = lambda *shape: pltpu.VMEM(shape, f32)
     dma = pltpu.SemaphoreType.DMA
@@ -602,15 +626,16 @@
         scratch_shapes=[
             vf(2, 2, 4, 32, 128), vf(rows, rows), v(*weight_in.shape), v(*weight_out.shape), vf(16, 128), v(2, width, 768), v(hidden, width),
             v(rows, width), v(rows, width), v(rows, 3 * width), v(rows, width), v(rows, width), vf(rows, width), v(rows, hidden),
-            v(2, rows, 768), vf(rows, width), vf(rows, width), dma((11, 10)), dma((11, 10)), dma((8,)), dma((13,))],
+            v(2, rows, 768), vf(rows, width), vf(rows, width), v(rows, width), vf(rows, width), v(rows, width), dma((11, 10)),
+            dma((11, 10)), dma((16,)), dma((13,)), dma((3, rows // 128))],
         compiler_params=pltpu.CompilerParams(collective_id=1, has_side_effects=True, vmem_limit_bytes=64 * 2**20 - 65536),
         name="forward",
     )(weight_in, weight_out, vectors, seg.reshape(1, rows), prev, tokens, grad_out)
 
 
 class Scatter:
-    def __init__(self, full, got, send_sem, recv_sem):
-        self.full, self.got = full, got
+    def __init__(self, routes, full, got, send_sem, recv_sem):
+        self.routes, self.full, self.got = routes, full, got
         self.send_sem, self.recv_sem = send_sem, recv_sem
         y, c, z, x = self.y, self.c, self.z, self.x = coords()
         first, second = (1 - y) * 2 + c, z * 2 + 1 - x
@@ -660,40 +685,72 @@
         for d in self.to_one(k):
             d.start()
 
+    def early_z(self, k):
+        full, (y, x) = self.full[k](), self.at_two
+        out = []
+        for i in range(3):
+            z = lax.rem(self.z + i + 1, 4)
+            who = dev(self.y, self.c, z, self.x)
+            out.append(self.copy(full.at[self.y, self.c, z, self.x], self.got[k][2].at[i, 0], k, 3 + 2 * i, who))
+            out.append(self.copy(full.at[y, self.c, z, x], self.got[k][2].at[i, 1], k, 4 + 2 * i, who))
+        return out
+
+    def last_two(self, k):
+        y, x = self.at_two
+        return self.copy(self.full[k]().at[y, self.c, self.z, x], self.got[k][3].at[0], k, 9, self.two)
+
+    def add(self, full, spot, *terms):
+        total = full[spot].astype(jnp.float32)
+        for t in terms:
+            total = total + t.astype(jnp.float32)
+        full[spot] = total.astype(full.dtype)
+
     def r3(self, k):
         full, got = self.full[k](), self.got[k][1]
         for d in self.to_one(k):
             d.wait_recv()
         y, x = self.at_two
+        straight = self.routes[k] == "z"
 
         @pl.loop(0, 4)
         def _(z):
-            total = full[y, self.c, z, x].astype(jnp.float32) + got[0, z].astype(jnp.float32)
-            full[y, self.c, z, x] = total.astype(full.dtype)
-        self.to_two(k).start()
+            self.add(full, (y, self.c, z, x), got[0, z])
+            if not straight:
+                self.add(full, (self.y, self.c, z, self.x), got[1, z])
+        for d in [self.to_two(k)] if straight else self.early_z(k):
+            d.start()
 
     def r4(self, k):
-        full = self.full[k]()
+        full, got = self.full[k](), self.got[k]
+        mine = (self.y, self.c, self.z, self.x)
+        if self.routes[k] == "n":
+            for d in self.early_z(k):
+                d.wait_recv()
+            y, x = self.at_two
+            self.add(full, (y, self.c, self.z, x), *[got[2][i, 1] for i in range(3)])
+            self.last_two(k).start()
+            self.add(full, mine, *[got[2][i, 0] for i in range(3)])
+            return
         self.to_two(k).wait_recv()
 
         @pl.loop(0, 4)
         def _(z):
-            total = full[self.y, self.c, z, self.x].astype(jnp.float32) + self.got[k][1][1, z].astype(jnp.float32)
-            total = total + self.got[k][2][z].astype(jnp.float32)
-            full[self.y, self.c, z, self.x] = total.astype(full.dtype)
+            self.add(full, (self.y, self.c, z, self.x), got[1][1, z], got[2][z])
         for d in self.along_z(k):
             d.start()
 
     def r5(self, k):
-        for d in self.along_z(k):
+        last = [self.last_two(k)] if self.routes[k] == "n" else self.along_z(k)
+        for d in last:
             d.wait_recv()
         total = self.full[k]()[self.y, self.c, self.z, self.x].astype(jnp.float32)
-        for i in range(3):
+        for i in range(len(last)):
             total = total + self.got[k][3][i].astype(jnp.float32)
         return total
 
     def finish(self, k):
-        for d in [self.to_core(k), *self.to_one(k), self.to_two(k), *self.along_z(k)]:
+        rest = [*self.early_z(k), self.last_two(k)] if self.routes[k] == "n" else [self.to_two(k), *self.along_z(k)]
+        for d in [self.to_core(k), *self.to_one(k), *rest]:
             d.wait_send()
 
 
@@ -714,7 +771,7 @@
             yield d, pltpu.roll(value[:, 128 * at:128 * (at + 2)], 256 - off, 1)[:, :128]
 
 
-def backward_kernel(heads, plan, columns, *refs):
+def backward_kernel(heads, plan, routes, columns, *refs):
     (ddown_ref, hlow_ref, small_ref, two_ref, sone_ref, probs_ref, dl_ref,
      act_hbm, gp_hbm, go_hbm, gu_hbm, gq_hbm, dsec_hbm, none_hbm, mixed_hbm, x_hbm, qkv_hbm,
      dprev_ref, dx_ref, gin_ref, gout_ref, gvec_ref, norm_ref) = refs[:23]
@@ -730,7 +787,7 @@
     got = [got_flat[4 * k:4 * k + 4] for k in range(14)]
     full = [lambda k=k: ups.at[k] for k in range(4)] + [lambda j=j: outs.at[j] for j in range(3)]
     full += [lambda p=p: ups.at[p // 2, :, :, :, :, :, :, pl.ds(384 * (p % 2), 384)] for p in range(6)] + [lambda: fvec_ref]
-    sc = Scatter(full, got, send_sem, recv_sem)
+    sc = Scatter(routes, full, got, send_sem, recv_sem)
     y, c, z, x = coords()
     peers = peers_of(y, c, z, x)
     stages = {1: sc.r1, 2: sc.r2, 3: sc.r3, 4: sc.r4}
@@ -957,7 +1014,7 @@
             share(i).wait_send()
 
 
-def backward_all(plan, columns, grad_down, hidden_low, small, two_sums, scale_one, probs, grad_logits,
+def backward_all(plan, routes, columns, grad_down, hidden_low, small, two_sums, scale_one, probs, grad_logits,
                  activated, slope, full_out, full_up, full_qkv, grad_second, normed_one, mixed, tokens, qkv):
     rows, width = tokens.shape
     heads = probs.shape[0]
@@ -968,16 +1025,17 @@
     hbm = pl.BlockSpec(memory_space=pl.ANY)
     r_in, r_out = full_qkv.shape[3] // 2, full_out.shape[3] // 2
     landing = []
-    for r, n in [(r_in, 768)] * 4 + [(r_out, 256)] * 3 + [(r_in, 384)] * 6:
-        landing += [pltpu.VMEM(lead + (r // 8, 8, n), bf16) for lead in ((2, 4, 2), (2, 4), (4,), (3,))]
-    landing += [pltpu.VMEM(lead + (16, 128), f32) for lead in ((2, 4, 2), (2, 4), (4,), (3,))]
+    kinds = [((r_in // 8, 8, 768), bf16)] * 4 + [((r_out // 8, 8, 256), bf16)] * 3 + [((r_in // 8, 8, 384), bf16)] * 6 + [((16, 128), f32)]
+    for (shape, kind), route in zip(kinds, routes):
+        rest = [(4,), (3,)] if route == "z" else [(3, 2), (1,)]
+        landing += [pltpu.VMEM(first + shape, kind) for first in [(2, 4, 2), (2, 4)] + rest]
     lead = (2, 2, 4, 2)
     v = lambda *shape: pltpu.VMEM(shape, bf16)
     vf = lambda *shape: pltpu.VMEM(shape, f32)
     shapes = [((r_in // 8, 8, 3 * width + hidden), f32), ((r_out // 8, 8, width), f32), ((16, 128), f32), ((8, 128), f32)]
     dma = pltpu.SemaphoreType.DMA
     return pl.pallas_call(
-        functools.partial(backward_kernel, heads, plan, columns),
+        functools.partial(backward_kernel, heads, plan, routes, columns),
         grid=(heads,),
         in_specs=[fixed((rows, width)), fixed((rows, width)), fixed(small.shape), fixed(two_sums.shape),
                   fixed(scale_one.shape), head, head] + [hbm] * 10,
@@ -988,7 +1046,7 @@
                         v(rows, 768), v(rows, 768), v(3, 768, width), vf(rows, width), vf(rows, width),
                         vf(16, width), vf(*lead, 16, 128)]
         + [v(4, *lead, r_in // 8, 8, 768), v(3, *lead, r_out // 8, 8, 256)] + landing
-        + [vf(2, 8, 128), vf(10, 8, 128), dma((14, 7)), dma((14, 7)), dma((10,)), dma((10,)), dma((10,))],
+        + [vf(2, 8, 128), vf(10, 8, 128), dma((14, 10)), dma((14, 10)), dma((10,)), dma((10,)), dma((10,))],
         compiler_params=pltpu.CompilerParams(collective_id=2, has_side_effects=True, vmem_limit_bytes=64 * 2**20 - 65536),
         name="backward",
     )(grad_down, hidden_low, small, two_sums, scale_one, probs, grad_logits,
@@ -1020,7 +1078,7 @@
 
 
 def update_all(norm, step_count, through, trios):
-    steps = 6
+    steps = 2
     f32 = jnp.float32
 
     def spec(a):
@@ -1106,11 +1164,11 @@
     sums = lambda v: jnp.sum(v, axis=0, dtype=jnp.float32)
     segments = segment_ids[0]
     if remote:
-        (logits, probs, full_qkv, full_up, full_out, qkv, mixed, hidden_low, normed_one, activated, slope, small, scale_one,
-         output, grad_second, grad_down, two_sums) = forward_all(
+        (logits, probs, full_qkv, full_up, full_out, qkv, mixed, hidden_low, normed_one, activated, slope, output, grad_second, grad_down,
+         small, scale_one, two_sums) = forward_all(
              FORWARD_PLAN, ROUTES, hidden_in, d_hidden, weight_in, weight_out, vectors, prev_logits[0], segments)
         grad_prev, grad_tokens, grad_in, grad_out, grad_vec, norm = backward_all(
-            BACKWARD_PLAN, vectors.shape[1], grad_down, hidden_low, small, two_sums, scale_one, probs, d_logits[0],
+            BACKWARD_PLAN, BACKWARD_ROUTES, vectors.shape[1], grad_down, hidden_low, small, two_sums, scale_one, probs, d_logits[0],
             activated, slope, full_out, full_up, full_qkv, grad_second, normed_one, mixed, hidden_in, qkv)
         (logits, grad_prev, output, grad_tokens, *states, grad_norm) = update_all(
             norm, step_count, [logits, grad_prev, output, grad_tokens],

time: 217 us -> 207 us (0.954)
  Pallas kernels: 215 us -> 205 us
    pallas_call x1, Pallas kernels: 105 us -> 98.4 us  [backward_all(): pl.pallas_call(functools.partial(backward_kernel, heads, plan, routes, co...]
where the time goes in v1:
time: 207 us
  Pallas kernels  205 us (99%)
    pallas_call x1, Pallas kernels, backward_all(): pl.pallas_call(functools.partial(backward_kernel, heads, plan, routes, co...  98.4 us
    pallas_call x1, Pallas kernels, forward_all(): pl.pallas_call(functools.partial(forward_kernel, plan, routes), grid=(hea...  91.1 us
    pallas_call x1, Pallas kernels, update_all(): pl.pallas_call(update_kernel, grid=(steps,), in_specs=[pl.BlockSpec((8, 1...  15.7 us

profile of v1, /device:TPU:0, one launch (start us, length us, event | category | flops | bytes accessed | tf_op | source)
XLA Modules:
  0.0 206.6 jit_solution(11869650820435404920)
XLA Ops:
  0.7 91.1 %forward.1 = (bf16[12,640,640]{2,1,0:T(8,128)(2,1)}, bf16[12,640,640]{2,1,0:T(8,128)(2,1)}, bf16[2,2,4,48,2304]{4,3,2,1,0:T(8,128)(2,1)}, bf16[2,2,4,48,3072]{4,...) custom-call(f32[24,5376]{1,0:T(8,128)} %refs_5_.1, ...), custom_call_target="tpu_custom_call" | custom-call | tf_op jit(solution)/shard_map/forward/pallas_call | solution.py:620
  91.8 98.4 %backward.1 = (bf16[12,640,640]{2,1,0:T(8,128)(2,1)}, bf16[640,768]{1,0:T(8,128)(2,1)}, f32[3,8,5376]{2,1,0:T(8,128)}, f32[15,8,768]{2,1,0:T(8,128)}, f32[16,128]{1,0:T(8,128)}, /*index=5*/f32[8,128]{1,0:T(8,128)}) custom-call(bf16[640,768]{1,0:T(8,128)(2,1)} %get-tuple-element.63.refs_0_, bf16[640,768]{1,0:T(8,128)(2,1)} %get-tuple-element.64.refs_1_, ...), custom_call_target="tpu_custom_call" | custom-call | tf_op jit(solution)/shard_map/backward/pallas_call | solution.py:1037
  190.8 15.7 %update.1 = (bf16[12,640,640]{2,1,0:T(8,128)(2,1)}, bf16[12,640,640]{2,1,0:T(8,128)(2,1)}, bf16[640,768]{1,0:T(8,128)(2,1)}, bf16[640,768]{1,0:T(8,128)(2,1)}, f...) custom-call(f32[8,128]{1,0:T(8,128)} %get-tuple-element.78.norm_ref,, ...), custom_call_target="tpu_custom_call" | custom-call | tf_op jit(solution)/shard_map/update/pallas_call | solution.py:1093

commit v2 on v1

--- a/solution.py
+++ b/solution.py
@@ -214,8 +214,8 @@
 ROUTES = "zzzzzzznnnn"
 BACKWARD_ROUTES = "nzzznzzzzznzzz"
 FORWARD_PLAN = {
-    "start": [(1, 7), (1, 8), (1, 9), (1, 10), (1, 0), (2, 0), (1, 1), (3, 0)],
-    ("q", 0): [(1, 2), (2, 1), (1, 3), (2, 2), (3, 1)],
+    "start": [(1, 0), (1, 1), (2, 0), (1, 7), (1, 8), (1, 9), (1, 10), (1, 2), (2, 1), (3, 0)],
+    ("q", 0): [(1, 3), (2, 2), (3, 1)],
     ("q", 1): [(2, 3), (1, 4), (3, 2)],
     ("q", 2): [(3, 3), (1, 5)],
     ("pair", 0): [(2, 4), (1, 6)],
@@ -891,9 +891,9 @@
         wo.start()
         late()[1].wait()
 
-        @pl.loop(0, rows // 128)
+        @pl.loop(0, rows // 64)
         def _(i):
-            sl = pl.ds(pl.multiple_of(i * 128, 128), 128)
+            sl = pl.ds(pl.multiple_of(i * 64, 64), 64)
             one, normed = acc_ref[sl, :], none_ref[sl, :]
             part_ref[0:1, :] += jnp.sum(one * normed, axis=0, keepdims=True)
             part_ref[2:3, :] += jnp.sum(one, axis=0, keepdims=True)

time: 207 us -> 206 us (level)
  no operation moved by 1% of the time
where the time goes in v2:
time: 206 us
  Pallas kernels  204 us (99%)
    pallas_call x1, Pallas kernels, backward_all(): pl.pallas_call(functools.partial(backward_kernel, heads, plan, routes, co...  97.6 us
    pallas_call x1, Pallas kernels, forward_all(): pl.pallas_call(functools.partial(forward_kernel, plan, routes), grid=(hea...  91.1 us
    pallas_call x1, Pallas kernels, update_all(): pl.pallas_call(update_kernel, grid=(steps,), in_specs=[pl.BlockSpec((8, 1...  15.7 us

profile of v2, /device:TPU:0, one launch (start us, length us, event | category | flops | bytes accessed | tf_op | source)
XLA Modules:
  0.0 205.9 jit_solution(6028502863344704567)
XLA Ops:
  0.7 91.1 %forward.1 = (bf16[12,640,640]{2,1,0:T(8,128)(2,1)}, bf16[12,640,640]{2,1,0:T(8,128)(2,1)}, bf16[2,2,4,48,2304]{4,3,2,1,0:T(8,128)(2,1)}, bf16[2,2,4,48,3072]{4,...) custom-call(f32[24,5376]{1,0:T(8,128)} %refs_5_.1, ...), custom_call_target="tpu_custom_call" | custom-call | tf_op jit(solution)/shard_map/forward/pallas_call | solution.py:620
  91.8 97.6 %backward.1 = (bf16[12,640,640]{2,1,0:T(8,128)(2,1)}, bf16[640,768]{1,0:T(8,128)(2,1)}, f32[3,8,5376]{2,1,0:T(8,128)}, f32[15,8,768]{2,1,0:T(8,128)}, f32[16,128]{1,0:T(8,128)}, /*index=5*/f32[8,128]{1,0:T(8,128)}) custom-call(bf16[640,768]{1,0:T(8,128)(2,1)} %get-tuple-element.63.refs_0_, bf16[640,768]{1,0:T(8,128)(2,1)} %get-tuple-element.64.refs_1_, ...), custom_call_target="tpu_custom_call" | custom-call | tf_op jit(solution)/shard_map/backward/pallas_call | solution.py:1037
  190.1 15.7 %update.1 = (bf16[12,640,640]{2,1,0:T(8,128)(2,1)}, bf16[12,640,640]{2,1,0:T(8,128)(2,1)}, bf16[640,768]{1,0:T(8,128)(2,1)}, bf16[640,768]{1,0:T(8,128)(2,1)}, f...) custom-call(f32[8,128]{1,0:T(8,128)} %get-tuple-element.78.norm_ref,, ...), custom_call_target="tpu_custom_call" | custom-call | tf_op jit(solution)/shard_map/update/pallas_call | solution.py:1093
